TPU v7x, 32 devices: a whole 2x2x4 slice. The times are simulated.
32 devices in a mesh: row: 4 (over y, x), col: 4 (over z), cores: 2 (over core).
Axes of the slice: x: 2, y: 2, z: 4, core: 2. Of those that a mesh axis runs over, the one named last changes fastest.
Arguments:
- multipoles: bfloat16 [315, 2048], P(None, ('col', 'row')), may hold values from -6 to 6
- operators: bfloat16 [40, 315, 315], P('cores'), may hold values from -0.0078125 to 0.0078125
- classes: int32 [2048, 2048], P('row', 'col'), may hold values from 0 to 39, as said below
- separated: int32 [4, 4], P('row', 'col'), may hold values 0 or 1
- owners: int32 [2048], P('row'), may hold values from 0 to 7, as said below
Outputs:
- owned: float32 [315, 4096], P(None, ('row', 'col', 'cores'))
Inputs may be any that keep to these rules, and one draw needn't show every extreme that they name: `owners`: in each block of 512 cells (cells b * 512 to b * 512 + 511) no owner holds more than 128 cells, and in every block one owner holds exactly 128. Cell t sits at (t % 8, (t // 8) % 4, t // 32) on a periodic grid of 8 x 4 x 2048 // 32 cells; classes[t, s] depends only on the wrapped offset between the positions of t and s.
All inputs are finite; a program needn't handle non-finite values. No bound on the sum of `separated` on one device may be relied on, other than what follows from the above.
Results may differ from a plain program's by a relative error of at most 0.0029.
Values may be sent and summed in bfloat16 or wider, within the bound.
A program may use at most 64 MiB of HBM per device.

v0:
```python
import jax
import jax.numpy as jnp
from jax import lax
from jax.sharding import PartitionSpec as P


def shards(multipoles, operators, classes, separated, owners):
    count = operators.shape[0]
    targets, sources = classes.shape
    base = lax.axis_index("cores") * count
    moved = jnp.einsum(
        "kqp,ps->kqs",
        operators,
        lax.all_gather(multipoles, "row", axis=1, tiled=True),
        preferred_element_type=jnp.float32,
    ).astype(jnp.bfloat16)
    spread = separated.shape[1]
    wide_mask = jnp.repeat(separated[0], sources // spread)
    labels = jnp.arange(count, dtype=jnp.int32) + base
    pick = (
        (classes[None, :, :] == labels[:, None, None]) & (wide_mask[None, None, :] == 1)
    ).astype(jnp.bfloat16)
    partial_value = jnp.einsum("kts,kqs->qt", pick, moved, preferred_element_type=jnp.float32)
    group = lax.axis_size(("col", "cores"))
    slots = 2 * targets // group
    member = lax.axis_index(("col", "cores"))
    hit = (owners[None, :] == jnp.arange(group, dtype=jnp.int32)[:, None]).astype(jnp.int32)
    before = jnp.cumsum(hit, axis=1) - hit
    rank = jnp.sum(before * hit, axis=0)
    slot_ids = jnp.arange(slots, dtype=jnp.int32)
    share = lax.psum_scatter(partial_value, ("col", "cores"), scatter_dimension=1, tiled=True)
    width = share.shape[1]
    share_owner = lax.dynamic_slice_in_dim(owners, member * width, width)
    outgoing = jnp.where(
        share_owner[None, None, :] == jnp.arange(group, dtype=jnp.int32)[:, None, None],
        share[None, :, :],
        0.0,
    )
    incoming = lax.all_to_all(outgoing, ("col", "cores"), split_axis=0, concat_axis=0, tiled=True)
    place = ((owners[None, :] == member) & (rank[None, :] == slot_ids[:, None])).astype(jnp.float32)
    owned = jnp.einsum(
        "spj,csj->pc", incoming, place.reshape(slots, group, width), precision=lax.Precision.HIGHEST
    )
    return owned


def solution(mesh):
    return jax.shard_map(
        shards,
        mesh=mesh,
        in_specs=(
            P(None, ("col", "row")),
            P("cores", None, None),
            P("row", "col"),
            P("row", "col"),
            P("row"),
        ),
        out_specs=P(None, ("row", "col", "cores")),
        check_vma=False,
    )
```

profile of v0, /device:TPU:0, one launch (start us, length us, event | category | flops | bytes accessed | tf_op | source)
XLA Modules:
  0.0 97.6 jit_solution(1368173200117882711)
XLA Ops:
  6.5 0.0 reduce-scatter.2.cloned.1.call-start
  6.5 11.0 %all_gather.3 = bf16[315,512]{1,0:T(8,128)(2,1)S(1)} all-gather(bf16[315,128]{1,0:T(8,128)(2,1)} %param.5), channel_id=1, replica_groups=mesh['row'=4,'col'=4,'cores'=2] {'row'}, dimensions={1}, use_global_device_ids=true | all-gather | bytes 403200 | tf_op jit(solution)/shard_map/all_gather | solution.py:14
  18.2 0.0 copy-start
  18.2 12.6 %fusion.6 = f32[315,512]{0,1:T(8,128)} fusion(s32[512,512]{1,0:T(8,128)} %param.7, s32[20]{0:T(128)S(1)} %iota_add_fusion, pred[]{:T(512)} %bitcast.1, bf16[20,315,315]{2,1,0:T(8,128)(2,1)} %param.6, bf16[315,512]{1,0:T(8,128)(2,1)S(1)} %all_gather.3), kind=kOutput, calls=%fused_computation.7 | convolution fusion | flops 5348853760 | bytes 5985337 | tf_op jit(solution)/shard_map/kts,kqs->qt/dot_general | solution.py:23
  30.8 0.0 reduce-scatter.2.cloned.1.call-update
  30.8 0.0 copy-done
  30.8 0.1 dynamic_slice.3
  30.9 31.8 %reduce-scatter.2.cloned.1.call-done = f32[315,64]{0,1:T(8,128)} async-done(((f32[315,512]{0,1:T(8,128)}), f32[315,64]{0,1:T(8,128)}) %reduce-scatter.2.cloned.1.call-update) | async-done | bytes 80656 | tf_op jit(solution)/shard_map/reduce_scatter | solution.py:31
  62.7 1.9 %broadcast_select_fusion = f32[8,315,64]{1,2,0:T(8,128)} fusion(f32[315,64]{0,1:T(8,128)} %reduce-scatter.2.cloned.1.call-done, pred[8,64]{1,0:T(8,128)(4,1)S(1)} %iota_compare_fusion.2), kind=kLoop, calls=%fused_computation.9 | loop fusion | flops 161280 | bytes 726272 | tf_op jit(solution)/shard_map/jit(_where)/select_n | solution.py:34
  64.7 3.5 %all-to-all-start = ((f32[8,315,64]{1,2,0:T(8,128)}), f32[8,315,64]{1,2,0:T(8,128)S(1)}, u32[]{:S(2)}, u32[]{:S(2)}) async-start(f32[8,315,64]{1,2,0:T(8,128)} %broadcast_select_fusion), calls=%async_computation.1 | async-start | bytes 1572864 | tf_op jit(solution)/shard_map/all_to_all | solution.py:39
  68.2 1.1 %reduce-window.6 = s32[8,4,128]{2,0,1:T(8,128)S(1)} reduce-window(s32[8,4,128]{2,0,1:T(8,128)S(1)} %fusion.15, s32[]{:T(128)} %constant.22.clone.1), window={size=1x1x128 pad=0_0x0_0x127_0}, to_apply=%region_1.2 | reduce-window | flops 520192 | bytes 32772 | tf_op jit(solution)/shard_map/reduce-window
  69.4 0.2 slice_reduce_fusion
  69.6 0.1 select_reduce_fusion
  69.7 0.1 eq.93
  69.8 0.1 and.23
  69.9 19.2 %all-to-all-done = f32[8,315,64]{1,2,0:T(8,128)S(1)} async-done(((f32[8,315,64]{1,2,0:T(8,128)}), f32[8,315,64]{1,2,0:T(8,128)S(1)}, u32[]{:S(2)}, u32[]{:S(2)}) %all-to-all-start) | async-done | bytes 645152 | tf_op jit(solution)/shard_map/all_to_all | solution.py:39
  89.1 1.6 %convolution_bitcast_fusion = f32[315,128]{1,0:T(8,128)} fusion(f32[8,315,64]{1,2,0:T(8,128)S(1)} %all-to-all-done, s32[8,64]{1,0:T(8,128)S(1)} %eq.93, pred[8,64]{1,0:T(8,128)(4,1)S(1)} %and.23), kind=kOutput, calls=%fused_computation.8 | convolution fusion | flops 247857152 | bytes 808960 | tf_op jit(solution)/shard_map/spj,csj->pc/dot_general | solution.py:41
  (6 shorter events, 0.1 us)
Async XLA Ops:
  6.5 56.2 %reduce-scatter.2.cloned.1.call-start = ((), (), s32[]{:S(2)}) async-start(), calls=%async_computation.2 | async-start | bytes 884736 | tf_op jit(solution)/shard_map/reduce_scatter | solution.py:31
  18.2 12.6 %copy-start = (s32[512]{0:T(512)S(1)}, s32[512]{0:T(512)}, u32[]{:S(2)}) copy-start(s32[512]{0:T(512)} %param.9) | copy-start | bytes 6148
  64.7 24.4 %all-to-all-start = ((f32[8,315,64]{1,2,0:T(8,128)}), f32[8,315,64]{1,2,0:T(8,128)S(1)}, u32[]{:S(2)}, u32[]{:S(2)}) async-start(f32[8,315,64]{1,2,0:T(8,128)} %broadcast_select_fusion), calls=%async_computation.1 | async-start | bytes 1572864 | tf_op jit(solution)/shard_map/all_to_all | solution.py:39
Sparse Core Ops, SparseCore 0:
  30.9 31.7 reduce-scatter.1
where the time goes:
time: 97.8 us; the launch traced here: 97.6 us
  waiting for transfers between devices  51.1 us (52%)
  matrix products  14.2 us (15%)
  between operations  14.1 us (14%)
  blocking collectives  11 us (11%)
  starting transfers between devices  3.55 us (4%)
  other arithmetic  3.2 us (3%)
    reduce_scatter x1, waiting for transfers between devices, shards(): lax.psum_scatter(partial_value, ('col', 'cores'), scatter_dimension=1, ti...  31.8 us
    all_to_all x1, waiting for transfers between devices, shards(): lax.all_to_all(outgoing, ('col', 'cores'), split_axis=0, concat_axis=0, t...  19.2 us
    dot_general x1, matrix products, shards(): jnp.einsum('kts,kqs->qt', pick, moved, preferred_element_type=jnp.float32)  12.6 us
    all_gather x1, blocking collectives, shards(): lax.all_gather(multipoles, 'row', axis=1, tiled=True)  11 us
    all_to_all x1, starting transfers between devices, shards(): lax.all_to_all(outgoing, ('col', 'cores'), split_axis=0, concat_axis=0, t...  3.55 us
  transfers between devices with their start and end apart: 2, of which 2 were waited for; matrix products, arithmetic and copies ran while one was open for 2% of the time, Pallas kernels for 0%

commit v1 on v0

--- a/solution.py
+++ b/solution.py
@@ -2,17 +2,35 @@
 import jax.numpy as jnp
 from jax import lax
 from jax.sharding import PartitionSpec as P
+from jax.lax import axis_index, ppermute, psum
 
 
 def shards(multipoles, operators, classes, separated, owners):
     count = operators.shape[0]
     targets, sources = classes.shape
     base = lax.axis_index("cores") * count
+
+    def _group_skins(packet):
+        nd = psum(1, "row")
+        left_arr = range(nd)
+        x_new = map(lambda t: (t, (t + 1) % nd), left_arr)
+        arrivals = list(x_new)
+        lower = range(nd)
+        y_new = map(lambda t: (t, (t - 1) % nd), lower)
+        in_order = list(y_new)
+        r1, answer = ([packet], [packet])
+        for _ in range(nd // 2):
+            reached = ppermute(r1[-1], "row", arrivals)
+            r1.append(reached)
+        for _ in tuple(range((nd - 1) // 2)):
+            inter = ppermute(answer[-1], "row", in_order)
+            answer.append(inter)
+        spare = jnp.concatenate([*r1[::-1], *answer[1:]], axis=1)
+        heard = axis_index("row")
+        return jnp.roll(spare, shift=(heard - nd // 2) * packet.shape[1], axis=1)
+
     moved = jnp.einsum(
-        "kqp,ps->kqs",
-        operators,
-        lax.all_gather(multipoles, "row", axis=1, tiled=True),
-        preferred_element_type=jnp.float32,
+        "kqp,ps->kqs", operators, _group_skins(multipoles), preferred_element_type=jnp.float32
     ).astype(jnp.bfloat16)
     spread = separated.shape[1]
     wide_mask = jnp.repeat(separated[0], sources // spread)

time: 97.8 us -> 101 us (1.033)
  blocking collectives: 11 us -> 0 us
  waiting for transfers between devices: 51.1 us -> 58.1 us
  starting transfers between devices: 3.55 us -> 8.85 us
  local copies, waits for them, and re-layouts: 0.47 us -> 2.42 us
    all_gather x1 -> x0, blocking collectives: 11 us -> none  [shards(): lax.all_gather(multipoles, 'row', axis=1, tiled=True)]
    ppermute x0 -> x3, waiting for transfers between devices: none -> 6.27 us  [the longest x2 6.27 us: _group_skins(): reached = ppermute(r1[-1], 'row', arrivals)]
    ppermute x0 -> x3, starting transfers between devices: none -> 5.3 us  [the longest x2 4.34 us: _group_skins(): reached = ppermute(r1[-1], 'row', arrivals)]
    unnamed x2 -> x9, local copies, waits for them, and re-layouts: 0.01 us -> 1.94 us
  transfers between devices with their start and end apart: 2 -> 5, of which waited for: 2 -> 4; matrix products, arithmetic and copies ran while one was open for 2% -> 3% of each run, Pallas kernels for 0% -> 0%
where the time goes in v1:
time: 101 us
  waiting for transfers between devices  58.1 us (58%)
  matrix products  14.2 us (14%)
  between operations  14.2 us (14%)
  starting transfers between devices  8.85 us (9%)
  other arithmetic  3.19 us (3%)
  local copies, waits for them, and re-layouts  2.42 us (2%)
    reduce_scatter x1, waiting for transfers between devices, shards(): lax.psum_scatter(partial_value, ('col', 'cores'), scatter_dimension=1, ti...  32.6 us
    all_to_all x1, waiting for transfers between devices, shards(): lax.all_to_all(outgoing, ('col', 'cores'), split_axis=0, concat_axis=0, t...  19.2 us
    dot_general x1, matrix products, shards(): jnp.einsum('kts,kqs->qt', pick, moved, preferred_element_type=jnp.float32)  12.6 us
    ppermute x2, waiting for transfers between devices, _group_skins(): reached = ppermute(r1[-1], 'row', arrivals)  6.27 us
    ppermute x2, starting transfers between devices, _group_skins(): reached = ppermute(r1[-1], 'row', arrivals)  4.34 us
    all_to_all x1, starting transfers between devices, shards(): lax.all_to_all(outgoing, ('col', 'cores'), split_axis=0, concat_axis=0, t...  3.55 us
  transfers between devices with their start and end apart: 5, of which 4 were waited for; matrix products, arithmetic and copies ran while one was open for 3% of the time, Pallas kernels for 0%

profile of v1, /device:TPU:0, one launch (start us, length us, event | category | flops | bytes accessed | tf_op | source)
XLA Modules:
  0.0 100.9 jit_solution(10613317040405938562)
XLA Ops:
  6.5 0.0 reduce-scatter.2.cloned.1.call-start
  6.5 2.9 %collective-permute-start = (bf16[315,128]{1,0:T(8,128)(2,1)}, bf16[315,128]{1,0:T(8,128)(2,1)S(1)}, u32[]{:S(2)}, u32[]{:S(2)}) collective-permute-start(bf16[315,128]{1,0:T(8,128)(2,1)} %param.5), channel_id=1, source_target_pairs={{0,8},{8,16},{16,24},{24,0},{1,9},{9,17},{17,25},{25,1},{2,10},{10... | collective-permute-start | bytes 241928 | tf_op jit(solution)/shard_map/ppermute | solution.py:23
  9.5 1.0 collective-permute-start.2
  11.1 2.3 %collective-permute-done = bf16[315,128]{1,0:T(8,128)(2,1)S(1)} collective-permute-done((bf16[315,128]{1,0:T(8,128)(2,1)}, bf16[315,128]{1,0:T(8,128)(2,1)S(1)}, u32[]{:S(2)}, u32[]{:S(2)}) %collective-permute-start) | collective-permute-done | bytes 80672 | tf_op jit(solution)/shard_map/ppermute | solution.py:23
  13.4 1.4 %collective-permute-start.1 = (bf16[315,128]{1,0:T(8,128)(2,1)S(1)}, bf16[315,128]{1,0:T(8,128)(2,1)S(1)}, u32[]{:S(2)}, u32[]{:S(2)}) collective-permute-start(bf16[315,128]{1,0:T(8,128)(2,1)S(1)} %collective-permute-done), channel_id=1, source_target_pairs={{0,8},{8,16},{16,24},{24,0},{1,9},{9,17},{17,25},{25,1},{2,10},{10... | collective-permute-start | bytes 241928 | tf_op jit(solution)/shard_map/ppermute | solution.py:23
  14.8 3.9 %collective-permute-done.1 = bf16[315,128]{1,0:T(8,128)(2,1)S(1)} collective-permute-done((bf16[315,128]{1,0:T(8,128)(2,1)S(1)}, bf16[315,128]{1,0:T(8,128)(2,1)S(1)}, u32[]{:S(2)}, u32[]{:S(2)}) %collective-permute-start.1) | collective-permute-done | bytes 80672 | tf_op jit(solution)/shard_map/ppermute | solution.py:23
  18.8 0.9 constant_dynamic-update-slice_fusion.5
  19.7 0.0 collective-permute-done.2
  19.8 0.9 constant_dynamic-update-slice_fusion.1
  20.8 0.0 copy-start
  20.8 12.6 %fusion.7 = f32[315,512]{0,1:T(8,128)} fusion(s32[512,512]{1,0:T(8,128)} %param.7, s32[20]{0:T(128)S(1)} %iota_add_fusion, pred[]{:T(512)} %bitcast.2, bf16[20,315,315]{2,1,0:T(8,128)(2,1)} %param.6, bf16[315,1024]{1,0:T(8,128)(2,1)S(1)} %constant_dynamic-update-slice_fusion, s32[]{:T(128)S(6)} %select_n.22), kind=kOutput, calls=%fused_computation.8 | convolution fusion | flops 5348853760 | bytes 5990893 | tf_op jit(solution)/shard_map/kts,kqs->qt/dot_general | solution.py:41
  33.4 0.0 reduce-scatter.2.cloned.1.call-update
  33.4 0.0 copy-done
  33.4 0.1 dynamic_slice.7
  33.5 32.6 %reduce-scatter.2.cloned.1.call-done = f32[315,64]{0,1:T(8,128)} async-done(((f32[315,512]{0,1:T(8,128)}), f32[315,64]{0,1:T(8,128)}) %reduce-scatter.2.cloned.1.call-update) | async-done | bytes 80656 | tf_op jit(solution)/shard_map/reduce_scatter | solution.py:49
  66.1 1.9 %broadcast_select_fusion = f32[8,315,64]{1,2,0:T(8,128)} fusion(f32[315,64]{0,1:T(8,128)} %reduce-scatter.2.cloned.1.call-done, pred[8,64]{1,0:T(8,128)(4,1)S(1)} %iota_compare_fusion.2), kind=kLoop, calls=%fused_computation.10 | loop fusion | flops 161280 | bytes 726272 | tf_op jit(solution)/shard_map/jit(_where)/select_n | solution.py:52
  68.0 3.5 %all-to-all-start = ((f32[8,315,64]{1,2,0:T(8,128)}), f32[8,315,64]{1,2,0:T(8,128)S(1)}, u32[]{:S(2)}, u32[]{:S(2)}) async-start(f32[8,315,64]{1,2,0:T(8,128)} %broadcast_select_fusion), calls=%async_computation.1 | async-start | bytes 1572864 | tf_op jit(solution)/shard_map/all_to_all | solution.py:57
  71.6 0.1 and.31
  71.7 1.1 %reduce-window.6 = s32[8,4,128]{2,0,1:T(8,128)S(1)} reduce-window(s32[8,4,128]{2,0,1:T(8,128)S(1)} %fusion.20, s32[]{:T(128)} %constant.45.clone.1), window={size=1x1x128 pad=0_0x0_0x127_0}, to_apply=%region_1.2 | reduce-window | flops 520192 | bytes 32772 | tf_op jit(solution)/shard_map/reduce-window
  72.8 0.2 slice_reduce_fusion
  73.1 0.1 select_reduce_fusion
  73.1 0.1 eq.96
  73.2 19.2 %all-to-all-done = f32[8,315,64]{1,2,0:T(8,128)S(1)} async-done(((f32[8,315,64]{1,2,0:T(8,128)}), f32[8,315,64]{1,2,0:T(8,128)S(1)}, u32[]{:S(2)}, u32[]{:S(2)}) %all-to-all-start) | async-done | bytes 645152 | tf_op jit(solution)/shard_map/all_to_all | solution.py:57
  92.5 1.6 %convolution_bitcast_fusion = f32[315,128]{1,0:T(8,128)} fusion(f32[8,315,64]{1,2,0:T(8,128)S(1)} %all-to-all-done, s32[8,64]{1,0:T(8,128)S(1)} %eq.96, pred[8,64]{1,0:T(8,128)(4,1)S(1)} %and.31), kind=kOutput, calls=%fused_computation.9 | convolution fusion | flops 247857152 | bytes 808960 | tf_op jit(solution)/shard_map/spj,csj->pc/dot_general | solution.py:59
  (12 shorter events, 0.2 us)
Async XLA Ops:
  6.5 59.6 %reduce-scatter.2.cloned.1.call-start = ((), (), s32[]{:S(2)}) async-start(), calls=%async_computation.2 | async-start | bytes 884736 | tf_op jit(solution)/shard_map/reduce_scatter | solution.py:49
  6.5 6.9 %collective-permute-start = (bf16[315,128]{1,0:T(8,128)(2,1)}, bf16[315,128]{1,0:T(8,128)(2,1)S(1)}, u32[]{:S(2)}, u32[]{:S(2)}) collective-permute-start(bf16[315,128]{1,0:T(8,128)(2,1)} %param.5), channel_id=1, source_target_pairs={{0,8},{8,16},{16,24},{24,0},{1,9},{9,17},{17,25},{25,1},{2,10},{10... | collective-permute-start | bytes 241928 | tf_op jit(solution)/shard_map/ppermute | solution.py:23
  9.5 10.3 %collective-permute-start.2 = (bf16[315,128]{1,0:T(8,128)(2,1)}, bf16[315,128]{1,0:T(8,128)(2,1)S(1)}, u32[]{:S(2)}, u32[]{:S(2)}) collective-permute-start(bf16[315,128]{1,0:T(8,128)(2,1)} %param.5), channel_id=1, source_target_pairs={{0,24},{8,0},{16,8},{24,16},{1,25},{9,1},{17,9},{25,17},{2,26},{10... | collective-permute-start | bytes 241928 | tf_op jit(solution)/shard_map/ppermute | solution.py:26
  13.4 5.3 %collective-permute-start.1 = (bf16[315,128]{1,0:T(8,128)(2,1)S(1)}, bf16[315,128]{1,0:T(8,128)(2,1)S(1)}, u32[]{:S(2)}, u32[]{:S(2)}) collective-permute-start(bf16[315,128]{1,0:T(8,128)(2,1)S(1)} %collective-permute-done), channel_id=1, source_target_pairs={{0,8},{8,16},{16,24},{24,0},{1,9},{9,17},{17,25},{25,1},{2,10},{10... | collective-permute-start | bytes 241928 | tf_op jit(solution)/shard_map/ppermute | solution.py:23
  20.8 12.6 %copy-start = (s32[512]{0:T(512)S(1)}, s32[512]{0:T(512)}, u32[]{:S(2)}) copy-start(s32[512]{0:T(512)} %param.9) | copy-start | bytes 6148
  68.0 24.4 %all-to-all-start = ((f32[8,315,64]{1,2,0:T(8,128)}), f32[8,315,64]{1,2,0:T(8,128)S(1)}, u32[]{:S(2)}, u32[]{:S(2)}) async-start(f32[8,315,64]{1,2,0:T(8,128)} %broadcast_select_fusion), calls=%async_computation.1 | async-start | bytes 1572864 | tf_op jit(solution)/shard_map/all_to_all | solution.py:57
Sparse Core Ops, SparseCore 0:
  33.5 32.5 reduce-scatter.1
